TPU v7x, 32 devices: a whole 2x2x4 slice. The times are simulated.
32 devices in a mesh: section: 2 (over core), dom: 16 (over z, y, x).
Axes of the slice: x: 2, y: 2, z: 4, core: 2. Of those that a mesh axis runs over, the one named last changes fastest.
Arguments:
- blocks: float32 [16, 32, 6, 128, 128], P('section', 'dom'), may hold values from -0.21875 to 0.21875
- column_index: int32 [16, 32, 6], P('section', 'dom'), may hold values from 0 to 31
- block_period: int32 [16, 32, 6], P('section', 'dom'), may hold values from 0 to 15, as said below
- cost_vector: float32 [16, 4096], P('section', 'dom'), may hold values from -6 to 6
- demand: float32 [16, 4096], P('section', 'dom'), may hold values from -12 to 12
- primal_start: float32 [16, 4096], P('section', 'dom'), may hold values from 0 to 2
- dual_start: float32 [16, 4096], P('section', 'dom'), may hold values from -3 to 3
- primal_weight: float32 [1], replicated, may hold values from 0.5 to 2
Outputs:
- primal_final: float32 [16, 4096], P('section', 'dom')
- dual_final: float32 [16, 4096], P('section', 'dom')
Inputs may be any that keep to these rules, and one draw needn't show every extreme that they name: block_period[p, r, k] is p or p - 1; it is p for k = 0 and for p = 0.
All inputs are finite; a program needn't handle non-finite values.
Results may differ from a plain program's by a relative error of at most 0.00011.
Values sent between devices are 32-bit elements; how exact they have to be, the bound alone decides.
A program may use at most 64 MiB of HBM per device.

v0:
```python
import jax
import jax.numpy as jnp
from jax import lax
from jax.sharding import PartitionSpec as P

step_scale = 0.4
epsilon = 1e-06


def passed_along(block, axis, distance):
    devices = range(lax.axis_size(axis))
    route = [(i - distance, i) for i in devices if i - distance in devices]
    return lax.ppermute(block, axis, route)


def slot_layout(column_index, block_period):
    periods_here = column_index.shape[0]
    local_period = jnp.arange(periods_here, dtype=jnp.int32)[:, None, None]
    global_period = lax.axis_index("section") * periods_here + local_period
    slot_index = local_period + block_period - global_period + 1
    return slot_index


def forward(blocks, column_index, slot_index, field):
    periods_here = field.shape[0]
    width_here = blocks.shape[-1]
    gathered = lax.all_gather(field, "dom", axis=1, tiled=True)
    carried = passed_along(gathered[-1:], "section", 1)
    stacked = jnp.concatenate([carried, gathered], axis=0)
    block_count = stacked.shape[1] // width_here
    picked = stacked.reshape(periods_here + 1, block_count, width_here)[slot_index, column_index]
    product = jnp.einsum("prkij,prkj->pri", blocks, picked, precision=lax.Precision.HIGHEST)
    return product.reshape(periods_here, -1)


def adjoint(blocks, column_index, slot_index, field):
    periods_here = field.shape[0]
    rows_here = blocks.shape[1]
    width_here = blocks.shape[-1]
    block_count = rows_here * lax.axis_size("dom")
    field_blocks = field.reshape(periods_here, rows_here, width_here)
    block_terms = jnp.einsum(
        "prkij,pri->prkj", blocks, field_blocks, precision=lax.Precision.HIGHEST
    )
    segment_ids = (slot_index * block_count + column_index).reshape(-1)
    dense_term = jax.ops.segment_sum(
        block_terms.reshape(-1, width_here),
        segment_ids,
        num_segments=(periods_here + 1) * block_count,
    )
    dense_term = dense_term.reshape(periods_here + 1, block_count * width_here)
    carried = passed_along(dense_term[:1], "section", -1)
    own_rows = dense_term[1:]
    merged = own_rows + jnp.concatenate([jnp.zeros_like(own_rows[:-1]), carried], axis=0)
    result = lax.psum_scatter(merged, "dom", scatter_dimension=1, tiled=True)
    return result


def on_device(
    blocks, column_index, block_period, cost_vector, demand, primal_start, dual_start, primal_weight
):
    slot_index = slot_layout(column_index, block_period)
    weight_now = primal_weight[0]
    tau_first = step_scale / weight_now
    sigma_first = step_scale * weight_now
    primal_one = jnp.maximum(
        0.0,
        primal_start
        - tau_first * (cost_vector - adjoint(blocks, column_index, slot_index, dual_start)),
    )
    dual_one = dual_start + sigma_first * (
        demand - forward(blocks, column_index, slot_index, 2.0 * primal_one - primal_start)
    )
    local_primal = jnp.sum((primal_one - primal_start) ** 2)
    local_dual = jnp.sum((dual_one - dual_start) ** 2)
    move_primal, move_dual = lax.psum((local_primal, local_dual), ("section", "dom"))
    weight_next = jnp.sqrt(weight_now * jnp.sqrt((move_dual + epsilon) / (move_primal + epsilon)))
    tau_second = step_scale / weight_next
    sigma_second = step_scale * weight_next
    primal_final = jnp.maximum(
        0.0,
        primal_one
        - tau_second * (cost_vector - adjoint(blocks, column_index, slot_index, dual_one)),
    )
    dual_final = dual_one + sigma_second * (
        demand - forward(blocks, column_index, slot_index, 2.0 * primal_final - primal_one)
    )
    return (primal_final, dual_final)


def solution(mesh):
    return jax.shard_map(
        on_device,
        mesh=mesh,
        in_specs=(
            P("section", "dom", None, None, None),
            P("section", "dom", None),
            P("section", "dom", None),
            P("section", "dom"),
            P("section", "dom"),
            P("section", "dom"),
            P("section", "dom"),
            P(),
        ),
        out_specs=(P("section", "dom"), P("section", "dom")),
        check_vma=False,
    )
```

profile of v0, /device:TPU:0, one launch (start us, length us, event | category | flops | bytes accessed | tf_op | source)
XLA Modules:
  0.0 288.4 jit_solution(15570511346201908841)
XLA Ops:
  7.2 0.7 fusion.14
  8.2 6.1 %fusion.10 = f32[8,2,1,6,128]{4,2,3,1,0:T(1,128)S(1)} fusion(f32[8,2,6,128,128]{4,3,2,1,0:T(8,128)} %param.8, f32[8,2,128,1,1]{2,0,1,3,4:T(8,128)} %bitcast.58), kind=kOutput, calls=%fused_computation.24 | convolution fusion | flops 18874368 | bytes 6348800 | tf_op jit(solution)/shard_map/prkij,pri->prkj/dot_general | solution.py:42
  14.3 0.9 scatter_custom_fusion
  15.2 1.3 collective-permute-start
  16.6 1.7 collective-permute-done
  18.3 0.7 pad_add_fusion.1
  19.8 78.9 %reduce-scatter.3.cloned.1.call-done = f32[8,256]{1,0:T(8,128)} async-done(((f32[8,4096]{1,0:T(8,128)}), f32[8,256]{1,0:T(8,128)}) %reduce-scatter.3.cloned.1.call-update) | async-done | bytes 8208 | tf_op jit(solution)/shard_map/reduce_scatter | solution.py:55
  98.7 1.3 multiply_reduce_fusion
  100.0 36.7 %all_gather.6 = f32[8,4096]{1,0:T(8,128)S(1)} all-gather(f32[8,256]{1,0:T(8,128)S(1)} %multiply_subtract_fusion.1), channel_id=1, replica_groups=mesh['section'=2,'dom'=16] {'dom'}, dimensions={1}, use_global_device_ids=true | all-gather | bytes 139264 | tf_op jit(solution)/shard_map/all_gather | solution.py:27
  136.7 1.3 collective-permute-start.1
  138.9 1.4 gather_fusion
  140.3 7.1 %fusion.18 = f32[8,2,1,128,1]{3,2,4,1,0:T(1,128)S(1)} fusion(f32[8,2,6,128,1]{3,4,2,1,0:T(1,128)S(1)} %bitcast.54, f32[8,2,6,128,128]{4,3,2,1,0:T(8,128)} %param.8), kind=kOutput, calls=%fused_computation.40 | convolution fusion | flops 18874368 | bytes 6348800 | tf_op jit(solution)/shard_map/prkij,prkj->pri/dot_general | solution.py:32
  147.4 0.7 multiply_reduce_fusion.1
  148.1 5.1 %fusion.8 = f32[8,2,1,6,128]{4,2,3,1,0:T(1,128)S(1)} fusion(f32[8,2,6,128,128]{4,3,2,1,0:T(8,128)} %param.8, f32[8,2,128,1,1]{2,0,1,3,4:T(8,128)S(1)} %bitcast.57), kind=kOutput, calls=%fused_computation.22 | convolution fusion | flops 18874368 | bytes 6348800 | tf_op jit(solution)/shard_map/prkij,pri->prkj/dot_general | solution.py:42
  153.2 0.9 scatter_custom_fusion.1
  154.1 1.3 collective-permute-start.2
  155.5 1.7 collective-permute-done.2
  157.9 37.2 %all-reduce.2 = (f32[]{:T(128)}, f32[]{:T(128)}) all-reduce(f32[]{:T(128)} %get-tuple-element.8, f32[]{:T(128)} %get-tuple-element.6), channel_id=1, replica_groups=mesh['section'=2,'dom'=16] {'section','dom'}, use_global_device_ids=true, to_apply=%region_3.0 | all-reduce | flops 2 | bytes 16 | tf_op jit(solution)/shard_map/psum | solution.py:76
  196.5 35.8 %reduce-scatter.5.cloned.1.call-done = f32[8,256]{1,0:T(8,128)} async-done(((f32[8,4096]{1,0:T(8,128)}), f32[8,256]{1,0:T(8,128)}) %reduce-scatter.5.cloned.1.call-update) | async-done | bytes 8208 | tf_op jit(solution)/shard_map/reduce_scatter | solution.py:55
  232.3 1.3 multiply_subtract_fusion
  233.6 36.6 %all_gather.7 = f32[8,4096]{1,0:T(8,128)S(1)} all-gather(f32[8,256]{1,0:T(8,128)S(1)} %get-tuple-element.4), channel_id=1, replica_groups=mesh['section'=2,'dom'=16] {'dom'}, dimensions={1}, use_global_device_ids=true | all-gather | bytes 139264 | tf_op jit(solution)/shard_map/all_gather | solution.py:27
  270.3 1.5 collective-permute-start.3
  272.5 1.4 gather_fusion.1
  273.9 7.1 %fusion.19 = f32[8,2,1,128,1]{3,2,4,1,0:T(1,128)S(1)} fusion(f32[8,2,6,128,1]{3,4,2,1,0:T(1,128)S(1)} %bitcast.53, f32[8,2,6,128,128]{4,3,2,1,0:T(8,128)} %param.8), kind=kOutput, calls=%fused_computation.41 | convolution fusion | flops 18874368 | bytes 6348800 | tf_op jit(solution)/shard_map/prkij,prkj->pri/dot_general | solution.py:32
  (40 shorter events, 3.4 us)
Async XLA Ops:
  7.2 91.5 %copy-start.1 = (f32[8,256]{1,0:T(8,128)S(1)}, f32[8,256]{1,0:T(8,128)}, u32[]{:S(2)}) copy-start(f32[8,256]{1,0:T(8,128)} %param.13) | copy-start | bytes 24580
  7.2 91.5 %copy-start.2 = (f32[8,256]{1,0:T(8,128)S(1)}, f32[8,256]{1,0:T(8,128)}, u32[]{:S(2)}) copy-start(f32[8,256]{1,0:T(8,128)} %param.11) | copy-start | bytes 24580
  7.2 91.5 %reduce-scatter.3.cloned.1.call-start = ((), (), s32[]{:S(2)}) async-start(), calls=%async_computation.2 | async-start | bytes 139264 | tf_op jit(solution)/shard_map/reduce_scatter | solution.py:55
  14.3 133.1 %copy-start = (f32[8,256]{1,0:T(8,128)S(1)}, f32[8,256]{1,0:T(8,128)}, u32[]{:S(2)}) copy-start(f32[8,256]{1,0:T(8,128)} %param.14) | copy-start | bytes 24580
  14.3 133.1 %copy-start.3 = (f32[8,256]{1,0:T(8,128)S(1)}, f32[8,256]{1,0:T(8,128)}, u32[]{:S(2)}) copy-start(f32[8,256]{1,0:T(8,128)} %param.12) | copy-start | bytes 24580
  15.2 3.1 %collective-permute-start = (f32[1,4096]{1,0:T(1,128)S(1)}, f32[1,4096]{1,0:T(1,128)S(1)}, u32[]{:S(2)}, u32[]{:S(2)}) collective-permute-start(f32[1,4096]{1,0:T(1,128)S(1)} %bitcast.59), channel_id=1, source_target_pairs={{16,0},{17,1},{18,2},{19,3},{20,4},{21,5},{22,6},{23,7},{24,8},{25... | collective-permute-start | bytes 49160 | tf_op jit(solution)/shard_map/ppermute | solution.py:13
  19.0 213.3 %reduce-scatter.5.cloned.1.call-start = ((), (), s32[]{:S(2)}) async-start(), calls=%async_computation.3 | async-start | bytes 139264 | tf_op jit(solution)/shard_map/reduce_scatter | solution.py:55
  136.7 2.1 collective-permute-start.1
  154.1 3.1 %collective-permute-start.2 = (f32[1,4096]{1,0:T(1,128)S(1)}, f32[1,4096]{1,0:T(1,128)S(1)}, u32[]{:S(2)}, u32[]{:S(2)}) collective-permute-start(f32[1,4096]{1,0:T(1,128)S(1)} %bitcast.60), channel_id=1, source_target_pairs={{16,0},{17,1},{18,2},{19,3},{20,4},{21,5},{22,6},{23,7},{24,8},{25... | collective-permute-start | bytes 49160 | tf_op jit(solution)/shard_map/ppermute | solution.py:13
  270.3 2.1 collective-permute-start.3
Sparse Core Ops, SparseCore 0:
  19.1 79.4 reduce-scatter.2
  158.0 74.2 reduce-scatter.4
where the time goes:
time: 289 us; the launch traced here: 288 us
  waiting for transfers between devices  119 us (41%)
  blocking collectives  110 us (38%)
  matrix products  25.4 us (9%)
  between operations  16.4 us (6%)
  other arithmetic  7.89 us (3%)
  starting transfers between devices  5.42 us (2%)
  local copies, waits for them, and re-layouts  3.43 us (1%)
    reduce_scatter x2, waiting for transfers between devices, adjoint(): result = lax.psum_scatter(merged, 'dom', scatter_dimension=1, tiled=True)  115 us
    all_gather x2, blocking collectives, forward(): gathered = lax.all_gather(field, 'dom', axis=1, tiled=True)  73.3 us
    psum x1, blocking collectives, on_device(): lax.psum((local_primal, local_dual), ('section', 'dom'))  37.2 us
    dot_general x2, matrix products, forward(): jnp.einsum('prkij,prkj->pri', blocks, picked, precision=lax.Precision.HIG...  14.2 us
    dot_general x2, matrix products, adjoint(): jnp.einsum('prkij,pri->prkj', blocks, field_blocks, precision=lax.Precisi...  11.2 us
  transfers between devices with their start and end apart: 6, of which 6 were waited for; matrix products, arithmetic and copies ran while one was open for 0% of the time, Pallas kernels for 0%

commit v1 on v0

--- a/solution.py
+++ b/solution.py
@@ -5,6 +5,16 @@
 
 step_scale = 0.4
 epsilon = 1e-06
+
+
+def ring_gather(x, axis, dim):
+    ways, here, hop = (lax.axis_size(axis), lax.axis_index(axis), x.shape[dim])
+    dims = [n * ways if d == dim else n for d, n in enumerate(x.shape)]
+    full = lax.dynamic_update_slice_in_dim(jnp.zeros(dims, x.dtype), x, here * hop, axis=dim)
+    for far in range(1, ways):
+        x = lax.ppermute(x, axis, [(d, (d + 1) % ways) for d in range(ways)])
+        full = lax.dynamic_update_slice_in_dim(full, x, (here - far) % ways * hop, axis=dim)
+    return full
 
 
 def passed_along(block, axis, distance):
@@ -24,7 +34,7 @@
 def forward(blocks, column_index, slot_index, field):
     periods_here = field.shape[0]
     width_here = blocks.shape[-1]
-    gathered = lax.all_gather(field, "dom", axis=1, tiled=True)
+    gathered = ring_gather(field, "dom", 1)
     carried = passed_along(gathered[-1:], "section", 1)
     stacked = jnp.concatenate([carried, gathered], axis=0)
     block_count = stacked.shape[1] // width_here

time: 289 us -> 432 us (1.49)
  waiting for transfers between devices: 119 us -> 335 us
  blocking collectives: 110 us -> 37.3 us
    ppermute x0 -> x30, waiting for transfers between devices: none -> 217 us  [ring_gather(): x = lax.ppermute(x, axis, [(d, (d + 1) % ways) for d in range(ways)])]
    all_gather x2 -> x0, blocking collectives: 73.3 us -> none  [forward(): gathered = lax.all_gather(field, 'dom', axis=1, tiled=True)]
  transfers between devices with their start and end apart: 6 -> 36, of which waited for: 6 -> 36; matrix products, arithmetic and copies ran while one was open for 0% -> 0% of each run, Pallas kernels for 0% -> 0%
where the time goes in v1:
time: 432 us; the launch traced here: 431 us
  waiting for transfers between devices  335 us (78%)
  blocking collectives  37.3 us (9%)
  matrix products  25.3 us (6%)
  between operations  16.8 us (4%)
  other arithmetic  7.86 us (2%)
  starting transfers between devices  5.38 us (1%)
    ppermute x30, waiting for transfers between devices, ring_gather(): x = lax.ppermute(x, axis, [(d, (d + 1) % ways) for d in range(ways)])  217 us
    reduce_scatter x2, waiting for transfers between devices, adjoint(): result = lax.psum_scatter(merged, 'dom', scatter_dimension=1, tiled=True)  113 us
    psum x1, blocking collectives, on_device(): lax.psum((local_primal, local_dual), ('section', 'dom'))  37.3 us
    dot_general x2, matrix products, forward(): jnp.einsum('prkij,prkj->pri', blocks, picked, precision=lax.Precision.HIG...  14.2 us
    dot_general x2, matrix products, adjoint(): jnp.einsum('prkij,pri->prkj', blocks, field_blocks, precision=lax.Precisi...  11.2 us
  transfers between devices with their start and end apart: 36, of which 36 were waited for; matrix products, arithmetic and copies ran while one was open for 0% of the time, Pallas kernels for 0%

profile of v1, /device:TPU:0, one launch (start us, length us, event | category | flops | bytes accessed | tf_op | source)
XLA Modules:
  0.0 431.2 jit_solution(10888004704596012410)
XLA Ops:
  19.9 78.8 %reduce-scatter.3.cloned.1.call-done = f32[8,256]{1,0:T(8,128)} async-done(((f32[8,4096]{1,0:T(8,128)}), f32[8,256]{1,0:T(8,128)}) %reduce-scatter.3.cloned.1.call-update) | async-done | bytes 8208 | tf_op jit(solution)/shard_map/reduce_scatter | solution.py:65
  107.3 7.2 %collective-permute-done.2 = f32[8,256]{1,0:T(8,128)S(1)} collective-permute-done((f32[8,256]{1,0:T(8,128)S(1)}, f32[8,256]{1,0:T(8,128)S(1)}, u32[]{:S(2)}, u32[]{:S(2)}) %collective-permute-start.2) | collective-permute-done | bytes 8224 | tf_op jit(solution)/shard_map/ppermute | solution.py:15
  114.6 7.2 %collective-permute-done.3 = f32[8,256]{1,0:T(8,128)S(1)} collective-permute-done((f32[8,256]{1,0:T(8,128)S(1)}, f32[8,256]{1,0:T(8,128)S(1)}, u32[]{:S(2)}, u32[]{:S(2)}) %collective-permute-start.3) | collective-permute-done | bytes 8224 | tf_op jit(solution)/shard_map/ppermute | solution.py:15
  121.8 7.2 %collective-permute-done.4 = f32[8,256]{1,0:T(8,128)S(1)} collective-permute-done((f32[8,256]{1,0:T(8,128)S(1)}, f32[8,256]{1,0:T(8,128)S(1)}, u32[]{:S(2)}, u32[]{:S(2)}) %collective-permute-start.4) | collective-permute-done | bytes 8224 | tf_op jit(solution)/shard_map/ppermute | solution.py:15
  129.1 7.2 %collective-permute-done.5 = f32[8,256]{1,0:T(8,128)S(1)} collective-permute-done((f32[8,256]{1,0:T(8,128)S(1)}, f32[8,256]{1,0:T(8,128)S(1)}, u32[]{:S(2)}, u32[]{:S(2)}) %collective-permute-start.5) | collective-permute-done | bytes 8224 | tf_op jit(solution)/shard_map/ppermute | solution.py:15
  143.6 7.2 %collective-permute-done.7 = f32[8,256]{1,0:T(8,128)S(1)} collective-permute-done((f32[8,256]{1,0:T(8,128)S(1)}, f32[8,256]{1,0:T(8,128)S(1)}, u32[]{:S(2)}, u32[]{:S(2)}) %collective-permute-start.7) | collective-permute-done | bytes 8224 | tf_op jit(solution)/shard_map/ppermute | solution.py:15
  150.8 7.2 %collective-permute-done.8 = f32[8,256]{1,0:T(8,128)S(1)} collective-permute-done((f32[8,256]{1,0:T(8,128)S(1)}, f32[8,256]{1,0:T(8,128)S(1)}, u32[]{:S(2)}, u32[]{:S(2)}) %collective-permute-start.8) | collective-permute-done | bytes 8224 | tf_op jit(solution)/shard_map/ppermute | solution.py:15
  158.1 7.2 %collective-permute-done.9 = f32[8,256]{1,0:T(8,128)S(1)} collective-permute-done((f32[8,256]{1,0:T(8,128)S(1)}, f32[8,256]{1,0:T(8,128)S(1)}, u32[]{:S(2)}, u32[]{:S(2)}) %collective-permute-start.9) | collective-permute-done | bytes 8224 | tf_op jit(solution)/shard_map/ppermute | solution.py:15
  165.3 7.2 %collective-permute-done.10 = f32[8,256]{1,0:T(8,128)S(1)} collective-permute-done((f32[8,256]{1,0:T(8,128)S(1)}, f32[8,256]{1,0:T(8,128)S(1)}, u32[]{:S(2)}, u32[]{:S(2)}) %collective-permute-start.10) | collective-permute-done | bytes 8224 | tf_op jit(solution)/shard_map/ppermute | solution.py:15
  172.6 7.2 %collective-permute-done.11 = f32[8,256]{1,0:T(8,128)S(1)} collective-permute-done((f32[8,256]{1,0:T(8,128)S(1)}, f32[8,256]{1,0:T(8,128)S(1)}, u32[]{:S(2)}, u32[]{:S(2)}) %collective-permute-start.11) | collective-permute-done | bytes 8224 | tf_op jit(solution)/shard_map/ppermute | solution.py:15
  179.8 7.2 %collective-permute-done.12 = f32[8,256]{1,0:T(8,128)S(1)} collective-permute-done((f32[8,256]{1,0:T(8,128)S(1)}, f32[8,256]{1,0:T(8,128)S(1)}, u32[]{:S(2)}, u32[]{:S(2)}) %collective-permute-start.12) | collective-permute-done | bytes 8224 | tf_op jit(solution)/shard_map/ppermute | solution.py:15
  187.1 7.2 %collective-permute-done.13 = f32[8,256]{1,0:T(8,128)S(1)} collective-permute-done((f32[8,256]{1,0:T(8,128)S(1)}, f32[8,256]{1,0:T(8,128)S(1)}, u32[]{:S(2)}, u32[]{:S(2)}) %collective-permute-start.13) | collective-permute-done | bytes 8224 | tf_op jit(solution)/shard_map/ppermute | solution.py:15
  194.3 7.2 %collective-permute-done.14 = f32[8,256]{1,0:T(8,128)S(1)} collective-permute-done((f32[8,256]{1,0:T(8,128)S(1)}, f32[8,256]{1,0:T(8,128)S(1)}, u32[]{:S(2)}, u32[]{:S(2)}) %collective-permute-start.14) | collective-permute-done | bytes 8224 | tf_op jit(solution)/shard_map/ppermute | solution.py:15
  201.6 7.2 %collective-permute-done.15 = f32[8,256]{1,0:T(8,128)S(1)} collective-permute-done((f32[8,256]{1,0:T(8,128)S(1)}, f32[8,256]{1,0:T(8,128)S(1)}, u32[]{:S(2)}, u32[]{:S(2)}) %collective-permute-start.15) | collective-permute-done | bytes 8224 | tf_op jit(solution)/shard_map/ppermute | solution.py:15
  230.0 37.3 %all-reduce.2 = (f32[]{:T(128)}, f32[]{:T(128)}) all-reduce(f32[]{:T(128)} %get-tuple-element.9, f32[]{:T(128)} %get-tuple-element.7), channel_id=1, replica_groups=mesh['section'=2,'dom'=16] {'section','dom'}, use_global_device_ids=true, to_apply=%region_3.4 | all-reduce | flops 2 | bytes 16 | tf_op jit(solution)/shard_map/psum | solution.py:86
  268.7 34.3 %reduce-scatter.5.cloned.1.call-done = f32[8,256]{1,0:T(8,128)} async-done(((f32[8,4096]{1,0:T(8,128)}), f32[8,256]{1,0:T(8,128)}) %reduce-scatter.5.cloned.1.call-update) | async-done | bytes 8208 | tf_op jit(solution)/shard_map/reduce_scatter | solution.py:65
  304.3 7.2 %collective-permute-done.18 = f32[8,256]{1,0:T(8,128)S(1)} collective-permute-done((f32[8,256]{1,0:T(8,128)S(1)}, f32[8,256]{1,0:T(8,128)S(1)}, u32[]{:S(2)}, u32[]{:S(2)}) %collective-permute-start.18) | collective-permute-done | bytes 8224 | tf_op jit(solution)/shard_map/ppermute | solution.py:15
  311.6 7.2 %collective-permute-done.19 = f32[8,256]{1,0:T(8,128)S(1)} collective-permute-done((f32[8,256]{1,0:T(8,128)S(1)}, f32[8,256]{1,0:T(8,128)S(1)}, u32[]{:S(2)}, u32[]{:S(2)}) %collective-permute-start.19) | collective-permute-done | bytes 8224 | tf_op jit(solution)/shard_map/ppermute | solution.py:15
  318.8 7.2 %collective-permute-done.20 = f32[8,256]{1,0:T(8,128)S(1)} collective-permute-done((f32[8,256]{1,0:T(8,128)S(1)}, f32[8,256]{1,0:T(8,128)S(1)}, u32[]{:S(2)}, u32[]{:S(2)}) %collective-permute-start.20) | collective-permute-done | bytes 8224 | tf_op jit(solution)/shard_map/ppermute | solution.py:15
  326.1 7.2 %collective-permute-done.21 = f32[8,256]{1,0:T(8,128)S(1)} collective-permute-done((f32[8,256]{1,0:T(8,128)S(1)}, f32[8,256]{1,0:T(8,128)S(1)}, u32[]{:S(2)}, u32[]{:S(2)}) %collective-permute-start.21) | collective-permute-done | bytes 8224 | tf_op jit(solution)/shard_map/ppermute | solution.py:15
  340.6 7.2 %collective-permute-done.23 = f32[8,256]{1,0:T(8,128)S(1)} collective-permute-done((f32[8,256]{1,0:T(8,128)S(1)}, f32[8,256]{1,0:T(8,128)S(1)}, u32[]{:S(2)}, u32[]{:S(2)}) %collective-permute-start.23) | collective-permute-done | bytes 8224 | tf_op jit(solution)/shard_map/ppermute | solution.py:15
  347.8 7.2 %collective-permute-done.24 = f32[8,256]{1,0:T(8,128)S(1)} collective-permute-done((f32[8,256]{1,0:T(8,128)S(1)}, f32[8,256]{1,0:T(8,128)S(1)}, u32[]{:S(2)}, u32[]{:S(2)}) %collective-permute-start.24) | collective-permute-done | bytes 8224 | tf_op jit(solution)/shard_map/ppermute | solution.py:15
  355.1 7.2 %collective-permute-done.25 = f32[8,256]{1,0:T(8,128)S(1)} collective-permute-done((f32[8,256]{1,0:T(8,128)S(1)}, f32[8,256]{1,0:T(8,128)S(1)}, u32[]{:S(2)}, u32[]{:S(2)}) %collective-permute-start.25) | collective-permute-done | bytes 8224 | tf_op jit(solution)/shard_map/ppermute | solution.py:15
  362.3 7.2 %collective-permute-done.26 = f32[8,256]{1,0:T(8,128)S(1)} collective-permute-done((f32[8,256]{1,0:T(8,128)S(1)}, f32[8,256]{1,0:T(8,128)S(1)}, u32[]{:S(2)}, u32[]{:S(2)}) %collective-permute-start.26) | collective-permute-done | bytes 8224 | tf_op jit(solution)/shard_map/ppermute | solution.py:15
  (130 shorter events, 111.9 us)
Async XLA Ops:
  7.2 91.5 %reduce-scatter.3.cloned.1.call-start = ((), (), s32[]{:S(2)}) async-start(), calls=%async_computation.2 | async-start | bytes 139264 | tf_op jit(solution)/shard_map/reduce_scatter | solution.py:65
  19.0 284.0 %reduce-scatter.5.cloned.1.call-start = ((), (), s32[]{:S(2)}) async-start(), calls=%async_computation.3 | async-start | bytes 139264 | tf_op jit(solution)/shard_map/reduce_scatter | solution.py:65
  100.0 7.3 %collective-permute-start.1 = (f32[8,256]{1,0:T(8,128)S(1)}, f32[8,256]{1,0:T(8,128)S(1)}, u32[]{:S(2)}, u32[]{:S(2)}) collective-permute-start(f32[8,256]{1,0:T(8,128)S(1)} %get-tuple-element.12), channel_id=1, source_target_pairs={{0,1},{1,2},{2,3},{3,4},{4,5},{5,6},{6,7},{7,8},{8,9},{9,10},{10,1... | collective-permute-start | bytes 24584 | tf_op jit(solution)/shard_map/ppermute | solution.py:15
  107.3 7.2 %collective-permute-start.2 = (f32[8,256]{1,0:T(8,128)S(1)}, f32[8,256]{1,0:T(8,128)S(1)}, u32[]{:S(2)}, u32[]{:S(2)}) collective-permute-start(f32[8,256]{1,0:T(8,128)S(1)} %collective-permute-done.1), channel_id=1, source_target_pairs={{0,1},{1,2},{2,3},{3,4},{4,5},{5,6},{6,7},{7,8},{8,9},{9,10},{10,1... | collective-permute-start | bytes 24584 | tf_op jit(solution)/shard_map/ppermute | solution.py:15
  114.6 7.2 %collective-permute-start.3 = (f32[8,256]{1,0:T(8,128)S(1)}, f32[8,256]{1,0:T(8,128)S(1)}, u32[]{:S(2)}, u32[]{:S(2)}) collective-permute-start(f32[8,256]{1,0:T(8,128)S(1)} %collective-permute-done.2), channel_id=1, source_target_pairs={{0,1},{1,2},{2,3},{3,4},{4,5},{5,6},{6,7},{7,8},{8,9},{9,10},{10,1... | collective-permute-start | bytes 24584 | tf_op jit(solution)/shard_map/ppermute | solution.py:15
  121.8 7.2 %collective-permute-start.4 = (f32[8,256]{1,0:T(8,128)S(1)}, f32[8,256]{1,0:T(8,128)S(1)}, u32[]{:S(2)}, u32[]{:S(2)}) collective-permute-start(f32[8,256]{1,0:T(8,128)S(1)} %collective-permute-done.3), channel_id=1, source_target_pairs={{0,1},{1,2},{2,3},{3,4},{4,5},{5,6},{6,7},{7,8},{8,9},{9,10},{10,1... | collective-permute-start | bytes 24584 | tf_op jit(solution)/shard_map/ppermute | solution.py:15
  129.1 7.2 %collective-permute-start.5 = (f32[8,256]{1,0:T(8,128)S(1)}, f32[8,256]{1,0:T(8,128)S(1)}, u32[]{:S(2)}, u32[]{:S(2)}) collective-permute-start(f32[8,256]{1,0:T(8,128)S(1)} %collective-permute-done.4), channel_id=1, source_target_pairs={{0,1},{1,2},{2,3},{3,4},{4,5},{5,6},{6,7},{7,8},{8,9},{9,10},{10,1... | collective-permute-start | bytes 24584 | tf_op jit(solution)/shard_map/ppermute | solution.py:15
  136.3 7.2 %collective-permute-start.6 = (f32[8,256]{1,0:T(8,128)S(1)}, f32[8,256]{1,0:T(8,128)S(1)}, u32[]{:S(2)}, u32[]{:S(2)}) collective-permute-start(f32[8,256]{1,0:T(8,128)S(1)} %collective-permute-done.5), channel_id=1, source_target_pairs={{0,1},{1,2},{2,3},{3,4},{4,5},{5,6},{6,7},{7,8},{8,9},{9,10},{10,1... | collective-permute-start | bytes 24584 | tf_op jit(solution)/shard_map/ppermute | solution.py:15
  143.6 7.2 %collective-permute-start.7 = (f32[8,256]{1,0:T(8,128)S(1)}, f32[8,256]{1,0:T(8,128)S(1)}, u32[]{:S(2)}, u32[]{:S(2)}) collective-permute-start(f32[8,256]{1,0:T(8,128)S(1)} %collective-permute-done.6), channel_id=1, source_target_pairs={{0,1},{1,2},{2,3},{3,4},{4,5},{5,6},{6,7},{7,8},{8,9},{9,10},{10,1... | collective-permute-start | bytes 24584 | tf_op jit(solution)/shard_map/ppermute | solution.py:15
  150.8 7.2 %collective-permute-start.8 = (f32[8,256]{1,0:T(8,128)S(1)}, f32[8,256]{1,0:T(8,128)S(1)}, u32[]{:S(2)}, u32[]{:S(2)}) collective-permute-start(f32[8,256]{1,0:T(8,128)S(1)} %collective-permute-done.7), channel_id=1, source_target_pairs={{0,1},{1,2},{2,3},{3,4},{4,5},{5,6},{6,7},{7,8},{8,9},{9,10},{10,1... | collective-permute-start | bytes 24584 | tf_op jit(solution)/shard_map/ppermute | solution.py:15
  158.1 7.2 %collective-permute-start.9 = (f32[8,256]{1,0:T(8,128)S(1)}, f32[8,256]{1,0:T(8,128)S(1)}, u32[]{:S(2)}, u32[]{:S(2)}) collective-permute-start(f32[8,256]{1,0:T(8,128)S(1)} %collective-permute-done.8), channel_id=1, source_target_pairs={{0,1},{1,2},{2,3},{3,4},{4,5},{5,6},{6,7},{7,8},{8,9},{9,10},{10,1... | collective-permute-start | bytes 24584 | tf_op jit(solution)/shard_map/ppermute | solution.py:15
  165.3 7.2 %collective-permute-start.10 = (f32[8,256]{1,0:T(8,128)S(1)}, f32[8,256]{1,0:T(8,128)S(1)}, u32[]{:S(2)}, u32[]{:S(2)}) collective-permute-start(f32[8,256]{1,0:T(8,128)S(1)} %collective-permute-done.9), channel_id=1, source_target_pairs={{0,1},{1,2},{2,3},{3,4},{4,5},{5,6},{6,7},{7,8},{8,9},{9,10},{10,1... | collective-permute-start | bytes 24584 | tf_op jit(solution)/shard_map/ppermute | solution.py:15
  172.6 7.2 %collective-permute-start.11 = (f32[8,256]{1,0:T(8,128)S(1)}, f32[8,256]{1,0:T(8,128)S(1)}, u32[]{:S(2)}, u32[]{:S(2)}) collective-permute-start(f32[8,256]{1,0:T(8,128)S(1)} %collective-permute-done.10), channel_id=1, source_target_pairs={{0,1},{1,2},{2,3},{3,4},{4,5},{5,6},{6,7},{7,8},{8,9},{9,10},{10,1... | collective-permute-start | bytes 24584 | tf_op jit(solution)/shard_map/ppermute | solution.py:15
  179.8 7.2 %collective-permute-start.12 = (f32[8,256]{1,0:T(8,128)S(1)}, f32[8,256]{1,0:T(8,128)S(1)}, u32[]{:S(2)}, u32[]{:S(2)}) collective-permute-start(f32[8,256]{1,0:T(8,128)S(1)} %collective-permute-done.11), channel_id=1, source_target_pairs={{0,1},{1,2},{2,3},{3,4},{4,5},{5,6},{6,7},{7,8},{8,9},{9,10},{10,1... | collective-permute-start | bytes 24584 | tf_op jit(solution)/shard_map/ppermute | solution.py:15
  187.1 7.2 %collective-permute-start.13 = (f32[8,256]{1,0:T(8,128)S(1)}, f32[8,256]{1,0:T(8,128)S(1)}, u32[]{:S(2)}, u32[]{:S(2)}) collective-permute-start(f32[8,256]{1,0:T(8,128)S(1)} %collective-permute-done.12), channel_id=1, source_target_pairs={{0,1},{1,2},{2,3},{3,4},{4,5},{5,6},{6,7},{7,8},{8,9},{9,10},{10,1... | collective-permute-start | bytes 24584 | tf_op jit(solution)/shard_map/ppermute | solution.py:15
  194.3 7.2 %collective-permute-start.14 = (f32[8,256]{1,0:T(8,128)S(1)}, f32[8,256]{1,0:T(8,128)S(1)}, u32[]{:S(2)}, u32[]{:S(2)}) collective-permute-start(f32[8,256]{1,0:T(8,128)S(1)} %collective-permute-done.13), channel_id=1, source_target_pairs={{0,1},{1,2},{2,3},{3,4},{4,5},{5,6},{6,7},{7,8},{8,9},{9,10},{10,1... | collective-permute-start | bytes 24584 | tf_op jit(solution)/shard_map/ppermute | solution.py:15
  201.5 7.2 %collective-permute-start.15 = (f32[8,256]{1,0:T(8,128)S(1)}, f32[8,256]{1,0:T(8,128)S(1)}, u32[]{:S(2)}, u32[]{:S(2)}) collective-permute-start(f32[8,256]{1,0:T(8,128)S(1)} %collective-permute-done.14), channel_id=1, source_target_pairs={{0,1},{1,2},{2,3},{3,4},{4,5},{5,6},{6,7},{7,8},{8,9},{9,10},{10,1... | collective-permute-start | bytes 24584 | tf_op jit(solution)/shard_map/ppermute | solution.py:15
  304.3 7.2 %collective-permute-start.18 = (f32[8,256]{1,0:T(8,128)S(1)}, f32[8,256]{1,0:T(8,128)S(1)}, u32[]{:S(2)}, u32[]{:S(2)}) collective-permute-start(f32[8,256]{1,0:T(8,128)S(1)} %get-tuple-element.5), channel_id=1, source_target_pairs={{0,1},{1,2},{2,3},{3,4},{4,5},{5,6},{6,7},{7,8},{8,9},{9,10},{10,1... | collective-permute-start | bytes 24584 | tf_op jit(solution)/shard_map/ppermute | solution.py:15
  311.6 7.2 %collective-permute-start.19 = (f32[8,256]{1,0:T(8,128)S(1)}, f32[8,256]{1,0:T(8,128)S(1)}, u32[]{:S(2)}, u32[]{:S(2)}) collective-permute-start(f32[8,256]{1,0:T(8,128)S(1)} %collective-permute-done.18), channel_id=1, source_target_pairs={{0,1},{1,2},{2,3},{3,4},{4,5},{5,6},{6,7},{7,8},{8,9},{9,10},{10,1... | collective-permute-start | bytes 24584 | tf_op jit(solution)/shard_map/ppermute | solution.py:15
  318.8 7.2 %collective-permute-start.20 = (f32[8,256]{1,0:T(8,128)S(1)}, f32[8,256]{1,0:T(8,128)S(1)}, u32[]{:S(2)}, u32[]{:S(2)}) collective-permute-start(f32[8,256]{1,0:T(8,128)S(1)} %collective-permute-done.19), channel_id=1, source_target_pairs={{0,1},{1,2},{2,3},{3,4},{4,5},{5,6},{6,7},{7,8},{8,9},{9,10},{10,1... | collective-permute-start | bytes 24584 | tf_op jit(solution)/shard_map/ppermute | solution.py:15
  326.1 7.2 %collective-permute-start.21 = (f32[8,256]{1,0:T(8,128)S(1)}, f32[8,256]{1,0:T(8,128)S(1)}, u32[]{:S(2)}, u32[]{:S(2)}) collective-permute-start(f32[8,256]{1,0:T(8,128)S(1)} %collective-permute-done.20), channel_id=1, source_target_pairs={{0,1},{1,2},{2,3},{3,4},{4,5},{5,6},{6,7},{7,8},{8,9},{9,10},{10,1... | collective-permute-start | bytes 24584 | tf_op jit(solution)/shard_map/ppermute | solution.py:15
  333.3 7.2 %collective-permute-start.22 = (f32[8,256]{1,0:T(8,128)S(1)}, f32[8,256]{1,0:T(8,128)S(1)}, u32[]{:S(2)}, u32[]{:S(2)}) collective-permute-start(f32[8,256]{1,0:T(8,128)S(1)} %collective-permute-done.21), channel_id=1, source_target_pairs={{0,1},{1,2},{2,3},{3,4},{4,5},{5,6},{6,7},{7,8},{8,9},{9,10},{10,1... | collective-permute-start | bytes 24584 | tf_op jit(solution)/shard_map/ppermute | solution.py:15
  340.6 7.2 %collective-permute-start.23 = (f32[8,256]{1,0:T(8,128)S(1)}, f32[8,256]{1,0:T(8,128)S(1)}, u32[]{:S(2)}, u32[]{:S(2)}) collective-permute-start(f32[8,256]{1,0:T(8,128)S(1)} %collective-permute-done.22), channel_id=1, source_target_pairs={{0,1},{1,2},{2,3},{3,4},{4,5},{5,6},{6,7},{7,8},{8,9},{9,10},{10,1... | collective-permute-start | bytes 24584 | tf_op jit(solution)/shard_map/ppermute | solution.py:15
  369.6 7.2 %collective-permute-start.27 = (f32[8,256]{1,0:T(8,128)S(1)}, f32[8,256]{1,0:T(8,128)S(1)}, u32[]{:S(2)}, u32[]{:S(2)}) collective-permute-start(f32[8,256]{1,0:T(8,128)S(1)} %collective-permute-done.26), channel_id=1, source_target_pairs={{0,1},{1,2},{2,3},{3,4},{4,5},{5,6},{6,7},{7,8},{8,9},{9,10},{10,1... | collective-permute-start | bytes 24584 | tf_op jit(solution)/shard_map/ppermute | solution.py:15
  (16 other events, 662.0 us)
Sparse Core Ops, SparseCore 0:
  19.1 79.4 reduce-scatter.2
  230.1 72.8 reduce-scatter.4
